TPU v7x, 256 devices: a whole 4x4x8 slice. The times are simulated.
256 devices in a mesh: ctx: 64 (over x, z, y_hi), tp: 4 (over y_lo, core).
Axes of the slice: x: 4, y: 4 (y_hi: 2, y_lo: 2; y = y_hi * 2 + y_lo), z: 8, core: 2. Of those that a mesh axis runs over, the one named last changes fastest.
Arguments:
- q_one: bfloat16 [16384, 4096], P('ctx', 'tp'), may hold values from -880 to 880
- k_one: bfloat16 [16384, 4096], P('ctx', 'tp'), may hold values from -6 to 6
- v_one: bfloat16 [16384, 4096], P('ctx', 'tp'), may hold values from -6 to 6
- q_two: bfloat16 [16384, 4096], P('ctx', 'tp'), may hold values from -6 to 6
- k_two: bfloat16 [16384, 4096], P('ctx', 'tp'), may hold values from -6 to 6
- short_taps: bfloat16 [3, 7, 256], P(None, None, 'tp'), may hold values from -2 to 2
- medium_taps: bfloat16 [128, 256], P(None, 'tp'), may hold values from -0.5 to 0.5
- long_taps: bfloat16 [256, 16384], P('tp', 'ctx'), may hold values from -0.046875 to 0.046875
- skip_gain: float32 [4096], P('tp'), may hold values from -4 to 4
- block_order: int32 [64], replicated, may hold values from 0 to 63, as said below
- prev_owner: int32 [64], replicated, may hold values from 0 to 63, as said below
Outputs:
- gated_out: bfloat16 [16384, 4096], P('ctx', 'tp')
Inputs may be any that keep to these rules, and one draw needn't show every extreme that they name: `block_order`: A permutation of the 64 sequence blocks over the devices of ctx. prev_owner[b] is the device d with block_order[d] = b - 1 for b > 0, and prev_owner[0] the device holding block 63.
All inputs are finite; a program needn't handle non-finite values.
Results may differ from a plain program's by a relative error of at most 0.008.
Values may be sent and summed in bfloat16 or wider, within the bound.
A program may use at most 128 MiB of HBM per device.

v0:
```python
import math
import jax
import jax.numpy as jnp
from jax import lax
from jax.sharding import PartitionSpec as P

EPSILON = 1e-06
HIGHEST = lax.Precision.HIGHEST


def rows_filter(signal, kernel_taps):
    flipped = kernel_taps[::-1][:, None, :]
    result = lax.conv_general_dilated(
        signal[None],
        flipped,
        (1,),
        "VALID",
        dimension_numbers=("NWC", "WIO", "NWC"),
        feature_group_count=signal.shape[1],
        preferred_element_type=jnp.float32,
    )
    return result[0]


def angle_table(first_len, second_len, period):
    first = jnp.arange(first_len, dtype=jnp.int32)
    second = jnp.arange(second_len, dtype=jnp.int32)
    angle = 2.0 * math.pi / period * (first[:, None] * second[None, :] % period).astype(jnp.float32)
    return (jnp.cos(angle), jnp.sin(angle))


def forward_spectrum(signal, half_outer, tables):
    outer_cos, outer_sin, twist_cos, twist_sin, inner_cos, inner_sin = tables
    real_a = jnp.einsum("kn,bnm->bkm", outer_cos[:, :half_outer], signal, precision=HIGHEST)
    imag_a = -jnp.einsum("kn,bnm->bkm", outer_sin[:, :half_outer], signal, precision=HIGHEST)
    real_b = real_a * twist_cos + imag_a * twist_sin
    imag_b = imag_a * twist_cos - real_a * twist_sin
    real_c = jnp.einsum("bkm,mj->bkj", real_b, inner_cos, precision=HIGHEST) + jnp.einsum(
        "bkm,mj->bkj", imag_b, inner_sin, precision=HIGHEST
    )
    imag_c = jnp.einsum("bkm,mj->bkj", imag_b, inner_cos, precision=HIGHEST) - jnp.einsum(
        "bkm,mj->bkj", real_b, inner_sin, precision=HIGHEST
    )
    return (real_c, imag_c)


def inverse_spectrum(real_p, imag_p, half_outer, tables):
    outer_cos, outer_sin, twist_cos, twist_sin, inner_cos, inner_sin = tables
    real_q = jnp.einsum("bkj,jm->bkm", real_p, inner_cos, precision=HIGHEST) - jnp.einsum(
        "bkj,jm->bkm", imag_p, inner_sin, precision=HIGHEST
    )
    imag_q = jnp.einsum("bkj,jm->bkm", imag_p, inner_cos, precision=HIGHEST) + jnp.einsum(
        "bkj,jm->bkm", real_p, inner_sin, precision=HIGHEST
    )
    real_r = real_q * twist_cos - imag_q * twist_sin
    imag_r = imag_q * twist_cos + real_q * twist_sin
    return jnp.einsum(
        "nk,bkm->bnm", outer_cos[:half_outer], real_r, precision=HIGHEST
    ) - jnp.einsum("nk,bkm->bnm", outer_sin[:half_outer], imag_r, precision=HIGHEST)


def long_mix(values, long_rows, gain_local, block_rows):
    channels, length = values.shape
    outer_len = length // block_rows
    inner_len = 2 * block_rows
    half_outer = outer_len // 2
    padded_len = 2 * length
    outer_cos, outer_sin = angle_table(outer_len, outer_len, outer_len)
    twist_cos, twist_sin = angle_table(outer_len, inner_len, padded_len)
    inner_cos, inner_sin = angle_table(inner_len, inner_len, inner_len)
    tables = (outer_cos, outer_sin, twist_cos, twist_sin, inner_cos, inner_sin)
    value_float = values.astype(jnp.float32)
    real_x, imag_x = forward_spectrum(
        value_float.reshape(channels, half_outer, inner_len), half_outer, tables
    )
    real_h, imag_h = forward_spectrum(
        long_rows.astype(jnp.float32).reshape(long_rows.shape[0], half_outer, inner_len),
        half_outer,
        tables,
    )
    group_size = channels // long_rows.shape[0]
    real_h = jnp.repeat(real_h, group_size, axis=0)
    imag_h = jnp.repeat(imag_h, group_size, axis=0)
    real_p = real_x * real_h - imag_x * imag_h
    imag_p = real_x * imag_h + imag_x * real_h
    long_part = inverse_spectrum(real_p, imag_p, half_outer, tables) / padded_len
    return (long_part.reshape(channels, length) + gain_local[:, None] * value_float).astype(
        jnp.bfloat16
    )


def per_device(
    q_one,
    k_one,
    v_one,
    q_two,
    k_two,
    short_taps,
    medium_taps,
    long_taps,
    skip_gain,
    block_order,
    prev_owner,
):
    block_rows, local_width = q_one.shape
    ctx_count = lax.axis_size("ctx")
    device_pos = lax.axis_index("ctx")
    group_size = local_width // short_taps.shape[2]
    short_lead = short_taps.shape[1] - 1
    medium_reach = medium_taps.shape[0] - 1
    lane_width = local_width // ctx_count
    full_width = local_width * lax.axis_size("tp")
    short_lanes = jnp.repeat(short_taps, group_size, axis=2)
    medium_lanes = jnp.repeat(medium_taps, group_size, axis=1)
    lane_start = device_pos * lane_width
    slots = jnp.arange(ctx_count, dtype=jnp.int32)
    holder = jnp.sum(jnp.where(block_order[None, :] == slots[:, None], slots[None, :], 0), axis=1)
    my_block = block_order[device_pos]
    source = prev_owner[my_block]
    end_span = short_lead + medium_reach
    k_end = rows_filter(k_one[block_rows - end_span :], short_lanes[1])
    v_end = rows_filter(v_one[block_rows - end_span :], short_lanes[2])
    z_end = (k_end * v_end).astype(jnp.bfloat16)

    def select_source(carry, pieces):
        count = pieces[0].shape[0]
        matches = jnp.arange(count, dtype=jnp.int32) == source
        return tuple(
            (
                partial_sum
                + jnp.sum(jnp.where(matches[:, None, None], piece.astype(jnp.float32), 0.0), axis=0)
                for partial_sum, piece in zip(carry, pieces)
            )
        )

    empty_tails = (
        jnp.zeros((short_lead, local_width), jnp.float32),
        jnp.zeros((short_lead, local_width), jnp.float32),
        jnp.zeros((short_lead, local_width), jnp.float32),
        jnp.zeros((medium_reach, local_width), jnp.float32),
    )
    fetched = select_source(
        empty_tails,
        (
            lax.all_gather(q_one[None, block_rows - short_lead :], "ctx", axis=0, tiled=True),
            lax.all_gather(k_one[None, block_rows - short_lead :], "ctx", axis=0, tiled=True),
            lax.all_gather(v_one[None, block_rows - short_lead :], "ctx", axis=0, tiled=True),
            lax.all_gather(z_end[None], "ctx", axis=0, tiled=True),
        ),
    )
    has_before = my_block > 0
    tail_rows = [jnp.where(has_before, piece, 0.0).astype(jnp.bfloat16) for piece in fetched]
    q_feat = rows_filter(jnp.concatenate([tail_rows[0], q_one], axis=0), short_lanes[0])
    k_feat = rows_filter(jnp.concatenate([tail_rows[1], k_one], axis=0), short_lanes[1])
    v_feat = rows_filter(jnp.concatenate([tail_rows[2], v_one], axis=0), short_lanes[2])
    z_one = (k_feat * v_feat).astype(jnp.bfloat16)
    medium = rows_filter(jnp.concatenate([tail_rows[3], z_one], axis=0), medium_lanes)
    mixed = q_feat * medium
    energy = lax.psum(jnp.sum(mixed * mixed, axis=1), "tp")
    v_two = (
        k_two.astype(jnp.float32) * mixed * lax.rsqrt(energy / full_width + EPSILON)[:, None]
    ).astype(jnp.bfloat16)
    lanes, long_rows = (
        lax.all_to_all(jnp.transpose(v_two), "ctx", split_axis=0, concat_axis=1, tiled=True),
        lax.all_to_all(long_taps, "ctx", split_axis=0, concat_axis=1, tiled=True),
    )
    values = jnp.take(lanes.reshape(lane_width, ctx_count, block_rows), holder, axis=1).reshape(
        lane_width, ctx_count * block_rows
    )
    gain_local = lax.dynamic_slice_in_dim(skip_gain, lane_start, lane_width)
    mixed_seq = long_mix(values, long_rows, gain_local, block_rows)
    device_major = jnp.take(
        mixed_seq.reshape(lane_width, ctx_count, block_rows), block_order, axis=1
    ).reshape(lane_width, ctx_count * block_rows)
    returned = lax.all_to_all(device_major, "ctx", split_axis=1, concat_axis=0, tiled=True)
    return (q_two.astype(jnp.float32) * jnp.transpose(returned).astype(jnp.float32)).astype(
        jnp.bfloat16
    )


def solution(mesh):
    in_specs = (
        P("ctx", "tp"),
        P("ctx", "tp"),
        P("ctx", "tp"),
        P("ctx", "tp"),
        P("ctx", "tp"),
        P(None, None, "tp"),
        P(None, "tp"),
        P("tp", "ctx"),
        P("tp"),
        P(),
        P(),
    )
    out_specs = P("ctx", "tp")
    return jax.shard_map(
        per_device, mesh=mesh, in_specs=in_specs, out_specs=out_specs, check_vma=False
    )
```

profile of v0, /device:TPU:2, one launch (start us, length us, event | category | flops | bytes accessed | tf_op | source)
XLA Modules:
  0.0 769.9 jit_solution(8870785793664506424)
XLA Ops:
  6.5 0.8 slice_bitcast_fusion.12
  8.4 1.0 slice_bitcast_fusion.1
  10.2 0.3 convolution_select_fusion.3
  10.6 0.4 fusion.30
  11.3 0.7 slice.87
  12.0 0.5 broadcast.312
  12.5 0.7 reduce.1
  13.2 0.6 reshape.284
  13.8 14.7 %all-to-all-start.1 = ((bf16[64,2,128]{2,1,0:T(2,128)(2,1)}), bf16[64,2,128]{2,1,0:T(2,128)(2,1)S(1)}, u32[]{:S(2)}, u32[]{:S(2)}) async-start(bf16[64,2,128]{2,1,0:T(2,128)(2,1)} %reshape.284), calls=%async_computation.1 | async-start | bytes 65536 | tf_op jit(solution)/shard_map/all_to_all | solution.py:165
  28.5 0.6 dynamic_slice.9
  31.7 0.6 dynamic_slice.10
  32.3 0.6 iota_compare_fusion.3
  33.0 170.4 %all-gather.3 = bf16[64,6,1024]{2,1,0:T(8,128)(2,1)S(1)} all-gather(bf16[1,6,1024]{2,1,0:T(8,128)(2,1)S(1)} %slice_bitcast_fusion.9), channel_id=2, replica_groups=mesh['ctx'=64,'tp'=4] {'ctx'}, dimensions={0}, use_global_device_ids=true | all-gather | bytes 798720 | tf_op jit(solution)/shard_map/all_gather | solution.py:145
  203.4 172.6 %all-gather.4 = bf16[64,6,1024]{2,1,0:T(8,128)(2,1)S(1)} all-gather(bf16[1,6,1024]{2,1,0:T(8,128)(2,1)S(1)} %slice_bitcast_fusion.8), channel_id=3, replica_groups=mesh['ctx'=64,'tp'=4] {'ctx'}, dimensions={0}, use_global_device_ids=true | all-gather | bytes 798720 | tf_op jit(solution)/shard_map/all_gather | solution.py:146
  376.1 183.0 %all-gather.5 = bf16[64,6,1024]{2,1,0:T(8,128)(2,1)S(1)} all-gather(bf16[1,6,1024]{2,1,0:T(8,128)(2,1)S(1)} %slice_bitcast_fusion.7), channel_id=4, replica_groups=mesh['ctx'=64,'tp'=4] {'ctx'}, dimensions={0}, use_global_device_ids=true | all-gather | bytes 798720 | tf_op jit(solution)/shard_map/all_gather | solution.py:147
  559.1 1.0 fusion.4
  560.5 0.3 copy.120
  561.2 0.3 copy.117
  561.6 0.6 convolution_select_fusion
  562.2 0.7 fusion.25
  562.9 0.3 copy.122
  563.8 0.3 copy.105
  564.5 0.7 rev.14
  565.2 0.6 convolution_select_fusion.2
  565.8 0.6 copy.107
  566.4 1.3 reshape.270
  567.8 0.8 rev.17
  568.6 1.1 copy.125
  569.7 1.3 dynamic_slice.11
  571.4 0.5 fusion.138
  572.0 0.7 compare_and_fusion
  572.9 0.3 convolution_bitcast_fusion
  573.2 7.4 select_reduce_fusion
  580.9 0.8 copy-done.3
  581.7 14.8 %fusion.32 = f32[1,256,1024]{2,0,1:T(1,128)S(1)} fusion(bf16[128,1,1024]{2,1,0:T(2,128)(2,1)S(1)} %copy-done.3, bf16[1,383,1024]{2,1,0:T(8,128)(2,1)S(1)} %maximum_bitcast_fusion, f32[1,264,1024]{2,0,1:T(1,128)S(1)} %reshape.270), kind=kOutput, calls=%fused_computation.55 | convolution fusion | flops 67371008 | bytes 3143680 | tf_op jit(solution)/shard_map/conv_general_dilated | solution.py:13
  596.7 5.8 psum.7
  602.5 1.2 fusion.82
  603.8 1.0 copy.126
  604.8 33.8 %all-to-all-start = ((bf16[64,16,256]{2,1,0:T(8,128)(2,1)}), bf16[64,16,256]{2,1,0:T(8,128)(2,1)S(1)}, u32[]{:S(2)}, u32[]{:S(2)}) async-start(bf16[64,16,256]{2,1,0:T(8,128)(2,1)} %bitcast.26), calls=%async_computation | async-start | bytes 1048576 | tf_op jit(solution)/shard_map/all_to_all | solution.py:164
  638.6 0.3 fusion.31
  638.9 5.1 fusion.90
  644.0 5.1 fusion.88
  649.1 5.3 convolution_add_fusion.2
  654.4 5.1 convolution_subtract_fusion.2
  659.6 0.6 gather_fusion
  660.7 1.1 fusion.151
  661.8 1.1 fusion.153
  663.0 7.9 %fusion.52 = f32[16,64,512]{2,1,0:T(8,128)S(1)} fusion(f32[16,512,64]{1,2,0:T(8,128)S(1)} %fusion.153, f32[16,512,64]{1,2,0:T(8,128)S(1)} %fusion.151, f32[64,512]{1,0:T(8,128)S(1)} %get-tuple-element.14, f32[64,512]{1,0:T(8,128)S(1)} %get-tuple-element.15), kind=kOutput, calls=%fused_computation.76 | convolution fusion | flops 3226992640 | bytes 6553600 | tf_op jit(solution)/shard_map/bkm,mj->bkj/dot_general | solution.py:38
  670.9 7.7 %fusion.50 = f32[16,64,512]{2,1,0:T(8,128)S(1)} fusion(f32[16,512,64]{1,2,0:T(8,128)S(1)} %fusion.153, f32[16,512,64]{1,2,0:T(8,128)S(1)} %fusion.151, f32[64,512]{1,0:T(8,128)S(1)} %get-tuple-element.14, f32[64,512]{1,0:T(8,128)S(1)} %get-tuple-element.15), kind=kOutput, calls=%fused_computation.74 | convolution fusion | flops 3226992640 | bytes 6553600 | tf_op jit(solution)/shard_map/bkm,mj->bkj/dot_general | solution.py:41
  678.6 7.6 convolution_add_fusion.1
  686.2 7.8 %convolution_subtract_fusion.1 = f32[16,64,512]{2,1,0:T(8,128)S(1)} fusion(f32[16,64,512]{2,1,0:T(8,128)S(1)} %fusion.50, f32[16,512,64]{1,2,0:T(8,128)S(1)} %fusion.153, f32[16,512,64]{1,2,0:T(8,128)S(1)} %fusion.151, f32[64,512]{1,0:T(8,128)S(1)} %get-tuple-element.14, f32[64,512]{1,0:T(8,128)S(1)} %get-tuple-element.15), kind=kOutput, calls=%fused_computation.27 | convolution fusion | flops 3227516928 | bytes 8650752 | tf_op jit(solution)/shard_map/bkm,mj->bkj/dot_general | solution.py:41
  694.0 7.5 fusion.46
  701.6 8.0 %fusion.48 = f32[16,64,512]{2,1,0:T(8,128)S(1)} fusion(f32[16,64,512]{2,1,0:T(8,128)S(1)} %convolution_subtract_fusion.1, f32[16,64,512]{2,1,0:T(8,128)S(1)} %convolution_add_fusion.1, f32[64,512]{1,0:T(8,128)S(1)} %convolution_subtract_fusion.2, f32[64,512]{1,0:T(8,128)S(1)} %convolution_add_fusion.2), kind=kOutput, calls=%fused_computation.72 | convolution fusion | flops 3226468352 | bytes 6553600 | tf_op jit(solution)/shard_map/bkj,jm->bkm/dot_general | solution.py:49
  709.5 7.7 %convolution_add_fusion = f32[16,64,512]{2,1,0:T(8,128)S(1)} fusion(f32[16,64,512]{2,1,0:T(8,128)S(1)} %fusion.46, f32[16,64,512]{2,1,0:T(8,128)S(1)} %convolution_subtract_fusion.1, f32[16,64,512]{2,1,0:T(8,128)S(1)} %convolution_add_fusion.1, f32[64,512]{1,0:T(8,128)S(1)} %convolution_subtract_fusion.2, f32[64,512]{1,0:T(8,128)S(1)} %convolution_add_fusion.2), kind=kOutput, calls=%fused_computation.25 | convolution fusion | flops 3226992640 | bytes 8650752 | tf_op jit(solution)/shard_map/bkj,jm->bkm/dot_general | solution.py:52
  717.3 7.5 convolution_subtract_fusion
  724.8 1.6 fusion.5
  726.4 1.7 fusion.22
  728.3 0.5 copy-done.7
  728.8 0.8 fusion.54
  729.6 0.6 gather_fusion.1
  730.2 0.9 select_bitcast_fusion
  731.1 12.8 %all-to-all-start.2 = ((bf16[16,64,256]{2,0,1:T(8,128)(2,1)}), bf16[16,64,256]{2,0,1:T(8,128)(2,1)S(1)}, u32[]{:S(2)}, u32[]{:S(2)}) async-start(bf16[16,64,256]{2,0,1:T(8,128)(2,1)} %select_bitcast_fusion), calls=%async_computation.2 | async-start | bytes 1048576 | tf_op jit(solution)/shard_map/all_to_all | solution.py:175
  744.1 17.6 %all-to-all-done.2 = bf16[16,64,256]{2,0,1:T(8,128)(2,1)S(1)} async-done(((bf16[16,64,256]{2,0,1:T(8,128)(2,1)}), bf16[16,64,256]{2,0,1:T(8,128)(2,1)S(1)}, u32[]{:S(2)}, u32[]{:S(2)}) %all-to-all-start.2) | async-done | bytes 524320 | tf_op jit(solution)/shard_map/all_to_all | solution.py:175
  761.9 1.0 copy.132
  (87 shorter events, 5.9 us)
Async XLA Ops:
  6.5 3.3 copy-start.1
  6.5 566.7 %all-gather.8.cloned.1.call-start = ((), (), s32[]{:S(2)}) async-start(), calls=%async_computation.3 | async-start | bytes 17039360 | tf_op jit(solution)/shard_map/all_gather | solution.py:148
  9.5 0.8 copy-start.11
  10.6 2.0 copy-start.5
  10.6 17.9 %copy-start.9 = (s32[64]{0:T(128)S(1)}, s32[64]{0:T(128)}, u32[]{:S(2)}) copy-start(s32[64]{0:T(128)} %param.22) | copy-start | bytes 772
  10.6 21.1 %copy-start.8 = (s32[64]{0:T(128)S(1)}, s32[64]{0:T(128)}, u32[]{:S(2)}) copy-start(s32[64]{0:T(128)} %param.23) | copy-start | bytes 772
  10.6 22.3 %copy-start = (bf16[256,1024]{1,0:T(8,128)(2,1)S(1)}, bf16[256,1024]{1,0:T(8,128)(2,1)}, u32[]{:S(2)}) copy-start(bf16[256,1024]{1,0:T(8,128)(2,1)} %param.15) | copy-start | bytes 1572868
  11.0 22.0 %copy-start.2 = (bf16[256,1024]{1,0:T(8,128)(2,1)S(1)}, bf16[256,1024]{1,0:T(8,128)(2,1)}, u32[]{:S(2)}) copy-start(bf16[256,1024]{1,0:T(8,128)(2,1)} %param.13) | copy-start | bytes 1572868
  13.8 558.9 %all-to-all-start.1 = ((bf16[64,2,128]{2,1,0:T(2,128)(2,1)}), bf16[64,2,128]{2,1,0:T(2,128)(2,1)S(1)}, u32[]{:S(2)}, u32[]{:S(2)}) async-start(bf16[64,2,128]{2,1,0:T(2,128)(2,1)} %reshape.284), calls=%async_computation.1 | async-start | bytes 65536 | tf_op jit(solution)/shard_map/all_to_all | solution.py:165
  561.0 0.7 copy-start.10
  565.8 2.0 copy-start.6
  580.6 1.0 copy-start.3
  604.8 54.8 %all-to-all-start = ((bf16[64,16,256]{2,1,0:T(8,128)(2,1)}), bf16[64,16,256]{2,1,0:T(8,128)(2,1)S(1)}, u32[]{:S(2)}, u32[]{:S(2)}) async-start(bf16[64,16,256]{2,1,0:T(8,128)(2,1)} %bitcast.26), calls=%async_computation | async-start | bytes 1048576 | tf_op jit(solution)/shard_map/all_to_all | solution.py:164
  728.1 0.7 copy-start.7
  729.6 14.3 %copy-start.4 = (bf16[256,1024]{1,0:T(8,128)(2,1)S(1)}, bf16[256,1024]{1,0:T(8,128)(2,1)}, u32[]{:S(2)}) copy-start(bf16[256,1024]{1,0:T(8,128)(2,1)} %param.16) | copy-start | bytes 1572868
  731.1 30.6 %all-to-all-start.2 = ((bf16[16,64,256]{2,0,1:T(8,128)(2,1)}), bf16[16,64,256]{2,0,1:T(8,128)(2,1)S(1)}, u32[]{:S(2)}, u32[]{:S(2)}) async-start(bf16[16,64,256]{2,0,1:T(8,128)(2,1)} %select_bitcast_fusion), calls=%async_computation.2 | async-start | bytes 1048576 | tf_op jit(solution)/shard_map/all_to_all | solution.py:175
Sparse Core Ops, SparseCore 0:
  12.1 213.6 all-gather.7
where the time goes:
time: 778 us; the launch traced here: 770 us
  blocking collectives  532 us (68%)
  matrix products  106 us (14%)
  starting transfers between devices  61.3 us (8%)
  local copies, waits for them, and re-layouts  20.6 us (3%)
  waiting for transfers between devices  17.7 us (2%)
  between operations  17 us (2%)
  other arithmetic  15.6 us (2%)
    all_gather x1, blocking collectives, per_device(): lax.all_gather(v_one[None, block_rows - short_lead:], 'ctx', axis=0, tile...  183 us
    all_gather x1, blocking collectives, per_device(): lax.all_gather(k_one[None, block_rows - short_lead:], 'ctx', axis=0, tile...  173 us
    all_gather x1, blocking collectives, per_device(): lax.all_gather(q_one[None, block_rows - short_lead:], 'ctx', axis=0, tile...  170 us
    all_to_all x1, starting transfers between devices, per_device(): lax.all_to_all(jnp.transpose(v_two), 'ctx', split_axis=0, concat_axis=1,...  33.8 us
    all_to_all x1, waiting for transfers between devices, per_device(): lax.all_to_all(device_major, 'ctx', split_axis=1, concat_axis=0, tiled=True)  17.6 us
    conv_general_dilated x6, matrix products, rows_filter(): lax.conv_general_dilated(signal[None], flipped, (1,), 'VALID', dimension_...  17.3 us
  transfers between devices with their start and end apart: 4, of which 1 were waited for; matrix products, arithmetic and copies ran while one was open for 5% of the time, Pallas kernels for 0%

commit v1 on v0

--- a/solution.py
+++ b/solution.py
@@ -143,7 +143,15 @@
         empty_tails,
         (
             lax.all_gather(q_one[None, block_rows - short_lead :], "ctx", axis=0, tiled=True),
-            lax.all_gather(k_one[None, block_rows - short_lead :], "ctx", axis=0, tiled=True),
+            jnp.concatenate(
+                lax.all_to_all(
+                    jnp.stack([k_one[None, block_rows - short_lead :]] * lax.axis_size("ctx")),
+                    "ctx",
+                    0,
+                    0,
+                ),
+                axis=0,
+            ),
             lax.all_gather(v_one[None, block_rows - short_lead :], "ctx", axis=0, tiled=True),
             lax.all_gather(z_end[None], "ctx", axis=0, tiled=True),
         ),

time: 778 us -> 635 us (0.82)
  blocking collectives: 532 us -> 365 us
  starting transfers between devices: 61.3 us -> 74 us
  local copies, waits for them, and re-layouts: 20.6 us -> 29.6 us
    all_gather x1 -> x0, blocking collectives: 173 us -> none  [per_device(): lax.all_gather(k_one[None, block_rows - short_lead:], 'ctx', axis=0, tile...]
    all_gather x1, blocking collectives: 170 us -> 186 us  [per_device(): lax.all_gather(q_one[None, block_rows - short_lead:], 'ctx', axis=0, tile...]
    all_to_all x0 -> x1, starting transfers between devices: none -> 12.7 us  [per_device(): lax.all_to_all(jnp.stack([k_one[None, block_rows - short_lead:]] * lax.ax...]
    all_gather x1, blocking collectives: 183 us -> 174 us  [per_device(): lax.all_gather(v_one[None, block_rows - short_lead:], 'ctx', axis=0, tile...]
  transfers between devices with their start and end apart: 4 -> 5, of which waited for: 1 -> 1; matrix products, arithmetic and copies ran while one was open for 5% -> 8% of each run, Pallas kernels for 0% -> 0%
where the time goes in v1:
time: 635 us; the launch traced here: 629 us
  blocking collectives  365 us (57%)
  matrix products  107 us (17%)
  starting transfers between devices  74 us (12%)
  local copies, waits for them, and re-layouts  29.6 us (5%)
  other arithmetic  18 us (3%)
  waiting for transfers between devices  17.8 us (3%)
  between operations  17.1 us (3%)
    all_gather x1, blocking collectives, per_device(): lax.all_gather(q_one[None, block_rows - short_lead:], 'ctx', axis=0, tile...  186 us
    all_gather x1, blocking collectives, per_device(): lax.all_gather(v_one[None, block_rows - short_lead:], 'ctx', axis=0, tile...  174 us
    all_to_all x1, starting transfers between devices, per_device(): lax.all_to_all(jnp.transpose(v_two), 'ctx', split_axis=0, concat_axis=1,...  33.8 us
    all_to_all x1, waiting for transfers between devices, per_device(): lax.all_to_all(device_major, 'ctx', split_axis=1, concat_axis=0, tiled=True)  17.8 us
    conv_general_dilated x6, matrix products, rows_filter(): lax.conv_general_dilated(signal[None], flipped, (1,), 'VALID', dimension_...  17.3 us
    all_to_all x1, starting transfers between devices, per_device(): lax.all_to_all(long_taps, 'ctx', split_axis=0, concat_axis=1, tiled=True)  14.7 us
    dot_general x2, matrix products, forward_spectrum(): jnp.einsum('bkm,mj->bkj', real_b, inner_sin, precision=HIGHEST)  13.6 us
    dot_general x2, matrix products, forward_spectrum(): jnp.einsum('bkm,mj->bkj', real_b, inner_cos, precision=HIGHEST)  13 us
  transfers between devices with their start and end apart: 5, of which 1 were waited for; matrix products, arithmetic and copies ran while one was open for 8% of the time, Pallas kernels for 0%

profile of v1, /device:TPU:2, one launch (start us, length us, event | category | flops | bytes accessed | tf_op | source)
XLA Modules:
  0.0 629.0 jit_solution(9239776286544149945)
XLA Ops:
  6.5 0.8 slice_bitcast_fusion.11
  8.4 1.0 slice_bitcast_fusion.1
  11.3 0.7 slice.87
  12.1 0.5 broadcast.314
  12.6 0.7 reduce.1
  13.2 0.6 reshape.284
  13.9 14.7 %all-to-all-start.2 = ((bf16[64,2,128]{2,1,0:T(2,128)(2,1)}), bf16[64,2,128]{2,1,0:T(2,128)(2,1)S(1)}, u32[]{:S(2)}, u32[]{:S(2)}) async-start(bf16[64,2,128]{2,1,0:T(2,128)(2,1)} %reshape.284), calls=%async_computation.2 | async-start | bytes 65536 | tf_op jit(solution)/shard_map/all_to_all | solution.py:173
  28.5 0.6 dynamic_slice.9
  31.4 2.5 rev.14
  33.9 0.8 rev.17
  34.7 1.1 copy.127
  36.4 0.6 dynamic_slice.10
  37.0 1.3 dynamic_slice.11
  38.4 0.6 pad_clamp_fusion.1
  39.0 0.6 pad_clamp_fusion
  39.9 0.5 fusion.138
  40.5 0.6 compare_and_fusion.1
  41.1 1.2 iota_compare_fusion.3
  42.3 1.1 stack.3
  43.4 12.7 %all-to-all-start = ((bf16[64,1,6,1024]{3,2,1,0:T(8,128)(2,1)}), bf16[64,1,6,1024]{3,2,1,0:T(8,128)(2,1)S(1)}, u32[]{:S(2)}, u32[]{:S(2)}) async-start(bf16[64,1,6,1024]{3,2,1,0:T(8,128)(2,1)} %stack.3), calls=%async_computation | async-start | bytes 2097152 | tf_op jit(solution)/shard_map/all_to_all | solution.py:147
  56.1 0.5 compare_and_fusion
  56.6 0.7 slice_bitcast_fusion.7
  57.4 0.7 slice_bitcast_fusion.8
  58.1 185.7 %all-gather.2 = bf16[64,6,1024]{2,1,0:T(8,128)(2,1)S(1)} all-gather(bf16[1,6,1024]{2,1,0:T(8,128)(2,1)S(1)} %slice_bitcast_fusion.8), channel_id=2, replica_groups=mesh['ctx'=64,'tp'=4] {'ctx'}, dimensions={0}, use_global_device_ids=true | all-gather | bytes 798720 | tf_op jit(solution)/shard_map/all_gather | solution.py:145
  243.8 173.9 %all-gather.3 = bf16[64,6,1024]{2,1,0:T(8,128)(2,1)S(1)} all-gather(bf16[1,6,1024]{2,1,0:T(8,128)(2,1)S(1)} %slice_bitcast_fusion.7), channel_id=3, replica_groups=mesh['ctx'=64,'tp'=4] {'ctx'}, dimensions={0}, use_global_device_ids=true | all-gather | bytes 798720 | tf_op jit(solution)/shard_map/all_gather | solution.py:155
  417.7 0.8 reshape.285
  418.5 0.8 reduce
  419.3 0.8 reshape.178
  420.1 0.9 convolution_bitcast_fusion
  421.0 1.7 fusion.4
  424.7 0.6 convolution_select_fusion
  425.4 0.7 fusion.25
  428.0 0.6 convolution_select_fusion.2
  428.6 0.6 copy.108
  429.3 2.3 reshape.270
  431.6 7.4 %select_reduce_fusion = bf16[127,1024]{1,0:T(8,128)(2,1)S(1)} fusion(bf16[64,127,1024]{2,1,0:T(8,128)(2,1)} %all-gather.6.cloned.1.call-done, pred[64]{0:T(512)(128)(4,1)S(1)} %copy-done.22), kind=kLoop, calls=%fused_computation.2 | loop fusion | flops 24839168 | bytes 16906304 | tf_op jit(solution)/shard_map/reduce_sum | solution.py:131
  439.3 1.0 copy-done.3
  440.4 14.8 %fusion.32 = f32[1,256,1024]{2,0,1:T(1,128)S(1)} fusion(bf16[128,1,1024]{2,1,0:T(2,128)(2,1)S(1)} %copy-done.6, bf16[1,383,1024]{2,1,0:T(8,128)(2,1)S(1)} %maximum_bitcast_fusion, f32[1,264,1024]{2,0,1:T(1,128)S(1)} %copy-done.3), kind=kOutput, calls=%fused_computation.55 | convolution fusion | flops 67371008 | bytes 3143680 | tf_op jit(solution)/shard_map/conv_general_dilated | solution.py:13
  455.4 5.8 psum.7
  461.4 1.0 copy.128
  462.4 33.8 %all-to-all-start.1 = ((bf16[64,16,256]{2,1,0:T(8,128)(2,1)}), bf16[64,16,256]{2,1,0:T(8,128)(2,1)S(1)}, u32[]{:S(2)}, u32[]{:S(2)}) async-start(bf16[64,16,256]{2,1,0:T(8,128)(2,1)} %bitcast.27), calls=%async_computation.1 | async-start | bytes 1048576 | tf_op jit(solution)/shard_map/all_to_all | solution.py:172
  496.6 5.1 fusion.90
  501.7 5.1 fusion.88
  506.8 5.3 convolution_add_fusion.2
  512.1 5.8 convolution_subtract_fusion.2
  517.9 0.8 gather_fusion
  519.3 1.1 fusion.151
  520.5 1.1 fusion.153
  521.6 7.9 %fusion.52 = f32[16,64,512]{2,1,0:T(8,128)S(1)} fusion(f32[16,512,64]{1,2,0:T(8,128)S(1)} %fusion.153, f32[16,512,64]{1,2,0:T(8,128)S(1)} %fusion.151, f32[64,512]{1,0:T(8,128)S(1)} %get-tuple-element.14, f32[64,512]{1,0:T(8,128)S(1)} %get-tuple-element.15), kind=kOutput, calls=%fused_computation.76 | convolution fusion | flops 3226992640 | bytes 6553600 | tf_op jit(solution)/shard_map/bkm,mj->bkj/dot_general | solution.py:38
  529.5 7.7 %fusion.50 = f32[16,64,512]{2,1,0:T(8,128)S(1)} fusion(f32[16,512,64]{1,2,0:T(8,128)S(1)} %fusion.153, f32[16,512,64]{1,2,0:T(8,128)S(1)} %fusion.151, f32[64,512]{1,0:T(8,128)S(1)} %get-tuple-element.14, f32[64,512]{1,0:T(8,128)S(1)} %get-tuple-element.15), kind=kOutput, calls=%fused_computation.74 | convolution fusion | flops 3226992640 | bytes 6553600 | tf_op jit(solution)/shard_map/bkm,mj->bkj/dot_general | solution.py:41
  537.2 7.6 %convolution_add_fusion.1 = f32[16,64,512]{2,1,0:T(8,128)S(1)} fusion(f32[16,64,512]{2,1,0:T(8,128)S(1)} %fusion.52, f32[16,512,64]{1,2,0:T(8,128)S(1)} %fusion.153, f32[16,512,64]{1,2,0:T(8,128)S(1)} %fusion.151, f32[64,512]{1,0:T(8,128)S(1)} %get-tuple-element.14, f32[64,512]{1,0:T(8,128)S(1)} %get-tuple-element.15), kind=kOutput, calls=%fused_computation.28 | convolution fusion | flops 3227516928 | bytes 8650752 | tf_op jit(solution)/shard_map/bkm,mj->bkj/dot_general | solution.py:38
  544.8 7.8 %convolution_subtract_fusion.1 = f32[16,64,512]{2,1,0:T(8,128)S(1)} fusion(f32[16,64,512]{2,1,0:T(8,128)S(1)} %fusion.50, f32[16,512,64]{1,2,0:T(8,128)S(1)} %fusion.153, f32[16,512,64]{1,2,0:T(8,128)S(1)} %fusion.151, f32[64,512]{1,0:T(8,128)S(1)} %get-tuple-element.14, f32[64,512]{1,0:T(8,128)S(1)} %get-tuple-element.15), kind=kOutput, calls=%fused_computation.27 | convolution fusion | flops 3227516928 | bytes 8650752 | tf_op jit(solution)/shard_map/bkm,mj->bkj/dot_general | solution.py:41
  552.7 7.5 %fusion.46 = f32[16,64,512]{2,1,0:T(8,128)S(1)} fusion(f32[16,64,512]{2,1,0:T(8,128)S(1)} %convolution_subtract_fusion.1, f32[16,64,512]{2,1,0:T(8,128)S(1)} %convolution_add_fusion.1, f32[64,512]{1,0:T(8,128)S(1)} %copy-done.5, f32[64,512]{1,0:T(8,128)S(1)} %convolution_add_fusion.2), kind=kOutput, calls=%fused_computation.70 | convolution fusion | flops 3226468352 | bytes 6553600 | tf_op jit(solution)/shard_map/bkj,jm->bkm/dot_general | solution.py:52
  560.2 8.0 %fusion.48 = f32[16,64,512]{2,1,0:T(8,128)S(1)} fusion(f32[16,64,512]{2,1,0:T(8,128)S(1)} %convolution_subtract_fusion.1, f32[16,64,512]{2,1,0:T(8,128)S(1)} %convolution_add_fusion.1, f32[64,512]{1,0:T(8,128)S(1)} %copy-done.5, f32[64,512]{1,0:T(8,128)S(1)} %convolution_add_fusion.2), kind=kOutput, calls=%fused_computation.72 | convolution fusion | flops 3226468352 | bytes 6553600 | tf_op jit(solution)/shard_map/bkj,jm->bkm/dot_general | solution.py:49
  568.2 7.7 %convolution_add_fusion = f32[16,64,512]{2,1,0:T(8,128)S(1)} fusion(f32[16,64,512]{2,1,0:T(8,128)S(1)} %fusion.46, f32[16,64,512]{2,1,0:T(8,128)S(1)} %convolution_subtract_fusion.1, f32[16,64,512]{2,1,0:T(8,128)S(1)} %convolution_add_fusion.1, f32[64,512]{1,0:T(8,128)S(1)} %copy-done.5, f32[64,512]{1,0:T(8,128)S(1)} %convolution_add_fusion.2), kind=kOutput, calls=%fused_computation.25 | convolution fusion | flops 3226992640 | bytes 8650752 | tf_op jit(solution)/shard_map/bkj,jm->bkm/dot_general | solution.py:52
  575.9 7.6 %convolution_subtract_fusion = f32[16,64,512]{2,1,0:T(8,128)S(1)} fusion(f32[16,64,512]{2,1,0:T(8,128)S(1)} %fusion.48, f32[16,64,512]{2,1,0:T(8,128)S(1)} %convolution_subtract_fusion.1, f32[16,64,512]{2,1,0:T(8,128)S(1)} %convolution_add_fusion.1, f32[64,512]{1,0:T(8,128)S(1)} %copy-done.5, f32[64,512]{1,0:T(8,128)S(1)} %convolution_add_fusion.2), kind=kOutput, calls=%fused_computation.26 | convolution fusion | flops 3226992640 | bytes 8650752 | tf_op jit(solution)/shard_map/bkj,jm->bkm/dot_general | solution.py:49
  583.5 1.6 fusion.5
  585.1 1.7 fusion.22
  587.4 0.8 fusion.54
  588.3 0.8 gather_fusion.1
  589.1 0.9 select_bitcast_fusion
  590.1 12.7 %all-to-all-start.3 = ((bf16[16,64,256]{2,0,1:T(8,128)(2,1)}), bf16[16,64,256]{2,0,1:T(8,128)(2,1)S(1)}, u32[]{:S(2)}, u32[]{:S(2)}) async-start(bf16[16,64,256]{2,0,1:T(8,128)(2,1)} %select_bitcast_fusion), calls=%async_computation.3 | async-start | bytes 1048576 | tf_op jit(solution)/shard_map/all_to_all | solution.py:183
  603.0 17.8 %all-to-all-done.3 = bf16[16,64,256]{2,0,1:T(8,128)(2,1)S(1)} async-done(((bf16[16,64,256]{2,0,1:T(8,128)(2,1)}), bf16[16,64,256]{2,0,1:T(8,128)(2,1)S(1)}, u32[]{:S(2)}, u32[]{:S(2)}) %all-to-all-start.3) | async-done | bytes 524320 | tf_op jit(solution)/shard_map/all_to_all | solution.py:183
  620.9 1.0 copy.134
  (125 shorter events, 10.0 us)
Async XLA Ops:
  6.5 3.3 copy-start.1
  6.5 425.1 %all-gather.6.cloned.1.call-start = ((), (), s32[]{:S(2)}) async-start(), calls=%async_computation.4 | async-start | bytes 17039360 | tf_op jit(solution)/shard_map/all_gather | solution.py:156
  8.4 2.2 copy-start.19
  9.5 0.8 copy-start.29
  10.6 2.0 copy-start.17
  10.6 17.9 %copy-start.27 = (s32[64]{0:T(128)S(1)}, s32[64]{0:T(128)}, u32[]{:S(2)}) copy-start(s32[64]{0:T(128)} %param.22) | copy-start | bytes 772
  11.0 22.9 %copy-start.18 = (bf16[128,64]{0,1:T(8,128)(2,1)S(1)}, bf16[128,64]{0,1:T(8,128)(2,1)}, u32[]{:S(2)}) copy-start(bf16[128,64]{0,1:T(8,128)(2,1)} %param.19) | copy-start | bytes 49156
  11.0 25.4 %copy-start.26 = (s32[64]{0:T(128)S(1)}, s32[64]{0:T(128)}, u32[]{:S(2)}) copy-start(s32[64]{0:T(128)} %param.23) | copy-start | bytes 772
  13.9 28.4 %all-to-all-start.2 = ((bf16[64,2,128]{2,1,0:T(2,128)(2,1)}), bf16[64,2,128]{2,1,0:T(2,128)(2,1)S(1)}, u32[]{:S(2)}, u32[]{:S(2)}) async-start(bf16[64,2,128]{2,1,0:T(2,128)(2,1)} %reshape.284), calls=%async_computation.2 | async-start | bytes 65536 | tf_op jit(solution)/shard_map/all_to_all | solution.py:173
  39.8 456.5 %copy-start.12 = (f32[64,64]{0,1:T(8,128)}, f32[64,64]{0,1:T(8,128)S(1)}, u32[]{:S(2)}) copy-start(f32[64,64]{0,1:T(8,128)S(1)} %fusion.155) | copy-start | bytes 49156
  39.9 380.1 %copy-start.9 = (f32[64,64]{0,1:T(8,128)}, f32[64,64]{0,1:T(8,128)S(1)}, u32[]{:S(2)}) copy-start(f32[64,64]{0,1:T(8,128)S(1)} %fusion.156) | copy-start | bytes 49156
  42.2 1.1 copy-start.15
  43.4 377.6 %all-to-all-start = ((bf16[64,1,6,1024]{3,2,1,0:T(8,128)(2,1)}), bf16[64,1,6,1024]{3,2,1,0:T(8,128)(2,1)S(1)}, u32[]{:S(2)}, u32[]{:S(2)}) async-start(bf16[64,1,6,1024]{3,2,1,0:T(8,128)(2,1)} %stack.3), calls=%async_computation | async-start | bytes 2097152 | tf_op jit(solution)/shard_map/all_to_all | solution.py:147
  421.0 1.7 copy-start
  422.8 1.0 copy-start.2
  424.0 0.7 copy-start.28
  424.7 0.7 copy-start.20
  426.1 1.0 copy-start.4
  427.3 0.7 copy-start.21
  429.2 2.4 copy-start.22
  439.1 1.2 copy-start.3
  439.1 1.4 copy-start.6
  440.4 20.8 %copy-start.8 = (bf16[256,1024]{1,0:T(8,128)(2,1)S(1)}, bf16[256,1024]{1,0:T(8,128)(2,1)}, u32[]{:S(2)}) copy-start(bf16[256,1024]{1,0:T(8,128)(2,1)} %param.17) | copy-start | bytes 1572868
  461.2 35.4 %copy-start.16 = (f32[1,64,512]{2,1,0:T(8,128)S(1)}, f32[1,64,512]{2,1,0:T(8,128)}, u32[]{:S(2)}) copy-start(f32[1,64,512]{2,1,0:T(8,128)} %convolution_bitcast_fusion) | copy-start | bytes 393220
  462.4 55.5 %all-to-all-start.1 = ((bf16[64,16,256]{2,1,0:T(8,128)(2,1)}), bf16[64,16,256]{2,1,0:T(8,128)(2,1)S(1)}, u32[]{:S(2)}, u32[]{:S(2)}) async-start(bf16[64,16,256]{2,1,0:T(8,128)(2,1)} %bitcast.27), calls=%async_computation.1 | async-start | bytes 1048576 | tf_op jit(solution)/shard_map/all_to_all | solution.py:172
  512.1 6.7 %copy-start.23 = (pred[64]{0:T(512)(128)(4,1)S(1)}, pred[64]{0:T(512)(128)(4,1)}, u32[]{:S(2)}) copy-start(pred[64]{0:T(512)(128)(4,1)} %compare_and_fusion.1) | copy-start | bytes 196
  517.9 1.4 copy-start.13
  519.1 1.3 copy-start.10
  544.8 7.8 %copy-start.5 = (f32[64,512]{1,0:T(8,128)S(1)}, f32[64,512]{1,0:T(8,128)}, u32[]{:S(2)}) copy-start(f32[64,512]{1,0:T(8,128)} %convolution_subtract_fusion.2) | copy-start | bytes 393220
  575.9 7.6 %copy-start.14 = (f32[64,64]{0,1:T(8,128)S(1)}, f32[64,64]{0,1:T(8,128)}, u32[]{:S(2)}) copy-start(f32[64,64]{0,1:T(8,128)} %copy-done.12) | copy-start | bytes 49156
  583.5 1.6 copy-start.11
  586.8 0.7 copy-start.25
  587.4 1.7 copy-start.24
  588.2 14.6 %copy-start.7 = (bf16[256,1024]{1,0:T(8,128)(2,1)S(1)}, bf16[256,1024]{1,0:T(8,128)(2,1)}, u32[]{:S(2)}) copy-start(bf16[256,1024]{1,0:T(8,128)(2,1)} %param.16) | copy-start | bytes 1572868
  590.1 30.8 %all-to-all-start.3 = ((bf16[16,64,256]{2,0,1:T(8,128)(2,1)}), bf16[16,64,256]{2,0,1:T(8,128)(2,1)S(1)}, u32[]{:S(2)}, u32[]{:S(2)}) async-start(bf16[16,64,256]{2,0,1:T(8,128)(2,1)} %select_bitcast_fusion), calls=%async_computation.3 | async-start | bytes 1048576 | tf_op jit(solution)/shard_map/all_to_all | solution.py:183
Sparse Core Ops, SparseCore 0:
  12.2 218.4 all-gather.5
